TPU v7x, 256 devices: a whole 4x4x8 slice. The times are simulated.
256 devices in a mesh: band: 32 (over z, y_lo, core), hid: 8 (over x, y_hi).
Axes of the slice: x: 4, y: 4 (y_hi: 2, y_lo: 2; y = y_hi * 2 + y_lo), z: 8, core: 2. Of those that a mesh axis runs over, the one named last changes fastest.
Arguments:
- pair: float32 [768, 768, 128], P('band', 'hid'), may hold values from -40 to 40
- residue_mask: int32 [768], replicated, may hold values 0 or 1
- hotspot: int32 [768], replicated, may hold values 0 or 1
- interface: int32 [768, 768], P('band', 'hid'), may hold values 0 or 1
- proj_weight: float32 [2, 128, 512], replicated, may hold values from -0.5 to 0.5
- gate_weight: float32 [2, 128, 128], replicated, may hold values from -0.5 to 0.5
- out_weight: float32 [2, 128, 128], replicated, may hold values from -0.5 to 0.5
Outputs:
- pair_out: float32 [768, 768, 128], P('band', 'hid')
All inputs are finite; a program needn't handle non-finite values. No bound on the sum of `interface` on one device may be relied on, other than what follows from the above.
Results may differ from a plain program's by a relative error of at most 0.0021.
Values may be sent and summed in bfloat16 or wider, within the bound.
No kernel may reach another device: no remote copies, remote signals or barrier semaphores. Data moves between devices by JAX's collectives and lax.ppermute only.
A program may use at most 128 MiB of HBM per device.

v0:
```python
import jax
import jax.numpy as jnp
from jax import lax
from jax.sharding import PartitionSpec as P

EPS = 1e-05
HIGH = lax.Precision.HIGHEST


def normalize(values):
    average = jnp.mean(values, axis=-1, keepdims=True)
    centred = values - average
    variance = jnp.mean(centred * centred, axis=-1, keepdims=True)
    return centred * lax.rsqrt(variance + EPS)


def project(state, edge, weight):
    normed = normalize(state)
    proj = jnp.einsum("rmc,cf->frm", normed, weight, precision=HIGH)
    width = weight.shape[1] // 4
    left = (edge * jax.nn.sigmoid(proj[width : 2 * width]) * proj[:width]).astype(jnp.bfloat16)
    right = (edge * jax.nn.sigmoid(proj[3 * width :]) * proj[2 * width : 3 * width]).astype(
        jnp.bfloat16
    )
    return (normed, left, right)


def outgoing(left, right):
    return lax.dot_general(
        left,
        lax.all_gather(right, "band", axis=1, tiled=True),
        (((2,), (2,)), ((0,), (0,))),
        preferred_element_type=jnp.float32,
    )


def incoming(left, right):
    columns = lax.all_to_all(left, "band", split_axis=2, concat_axis=1, tiled=True)
    return lax.dot_general(
        columns,
        lax.all_gather(right, "band", axis=1, tiled=True),
        (((1,), (1,)), ((0,), (0,))),
        preferred_element_type=jnp.float32,
    )


def finish(tri, normed, gate_w, out_w):
    gating = jax.nn.sigmoid(jnp.einsum("rmd,dc->rmc", normed, gate_w, precision=HIGH))
    gathered = lax.all_to_all(tri, "hid", split_axis=2, concat_axis=0, tiled=True)
    average = jnp.mean(gathered, axis=0)
    variance = jnp.mean(gathered * gathered, axis=0) - average * average
    scaled = (gathered - average) * lax.rsqrt(variance + EPS)
    projected = jnp.einsum("hrm,hc->rmc", scaled, out_w, precision=HIGH)
    return gating * projected


def on_device(pair, residue_mask, hotspot, interface, proj_weight, gate_weight, out_weight):
    rows = pair.shape[0]
    cols = pair.shape[1]
    row_start = lax.axis_index("band") * rows
    col_start = lax.axis_index("hid") * cols
    row_mask = lax.dynamic_slice_in_dim(residue_mask, row_start, rows, 0)
    col_mask = lax.dynamic_slice_in_dim(residue_mask, col_start, cols, 0)
    row_hot = lax.dynamic_slice_in_dim(hotspot, row_start, rows, 0)
    col_hot = lax.dynamic_slice_in_dim(hotspot, col_start, cols, 0)
    flags = jnp.maximum(interface, jnp.maximum(row_hot[:, None], col_hot[None, :]))
    edge = (row_mask[:, None] * col_mask[None, :] * flags).astype(jnp.float32)
    state = pair
    for layer in range(2):
        normed, left, right = project(state, edge, proj_weight[layer])
        left, right = (
            lax.all_to_all(left, "hid", split_axis=0, concat_axis=2, tiled=True),
            lax.all_to_all(right, "hid", split_axis=0, concat_axis=2, tiled=True),
        )
        if layer == 0:
            tri = outgoing(left, right)
        else:
            tri = incoming(left, right)
        state = state + finish(tri, normed, gate_weight[layer], out_weight[layer])
    return state


def solution(mesh):
    return jax.shard_map(
        on_device,
        mesh=mesh,
        in_specs=(P("band", "hid", None), P(), P(), P("band", "hid"), P(), P(), P()),
        out_specs=P("band", "hid", None),
        check_vma=False,
    )
```

profile of v0, /device:TPU:96, one launch (start us, length us, event | category | flops | bytes accessed | tf_op | source)
XLA Modules:
  0.0 439.6 jit_solution(17324085471123526692)
XLA Ops:
  17.6 20.8 %all_to_all.120 = bf16[128,24,96]{2,1,0:T(8,128)(2,1)S(1)} all-to-all(bf16[128,24,96]{2,1,0:T(8,128)(2,1)S(1)} %copy.28), channel_id=1, replica_groups=mesh['band'=32,'hid'=8] {'hid'}, dimensions={0} | all-to-all | bytes 1179648 | tf_op jit(solution)/shard_map/all_to_all | solution.py:73
  40.8 16.0 %all_to_all.121 = bf16[128,24,96]{2,1,0:T(8,128)(2,1)S(1)} all-to-all(bf16[128,24,96]{2,1,0:T(8,128)(2,1)S(1)} %copy.26), channel_id=1, replica_groups=mesh['band'=32,'hid'=8] {'hid'}, dimensions={0} | all-to-all | bytes 1179648 | tf_op jit(solution)/shard_map/all_to_all | solution.py:72
  58.0 92.1 %all-gather.3.cloned.1.call-done = bf16[16,768,768]{2,1,0:T(8,128)(2,1)} async-done(((bf16[16,24,768]{2,1,0:T(8,128)(2,1)}), bf16[16,768,768]{2,1,0:T(8,128)(2,1)}) %all-gather.3.cloned.1.call-update) | async-done | bytes 18874384 | tf_op jit(solution)/shard_map/all_gather | solution.py:31
  150.1 8.9 %fusion.75 = f32[16,24,768]{2,1,0:T(8,128)S(1)} fusion(bf16[16,24,768]{2,1,0:T(8,128)(2,1)S(1)} %all_to_all.90, bf16[16,768,768]{2,1,0:T(8,128)(2,1)} %all-gather.3.cloned.1.call-done), kind=kOutput, calls=%fused_computation.96 | convolution fusion | flops 452984832 | bytes 20643840 | tf_op jit(solution)/shard_map/dot_general | solution.py:29
  159.0 5.0 %copy.30 = f32[16,24,768]{1,0,2:T(8,128)} copy(f32[16,24,768]{2,1,0:T(8,128)S(1)} %fusion.75) | data formatting | bytes 2359296 | tf_op jit(solution)/shard_map/dot_general | solution.py:29
  164.0 7.4 %reshape.61 = f32[8,1,36864]{2,1,0:T(1,128)} reshape(f32[768,16,24]{2,1,0:T(8,128)} %bitcast.87) | data formatting | bytes 2359296
  171.4 6.8 %all-to-all-start.2 = ((f32[8,1,36864]{2,1,0:T(1,128)}), f32[8,1,36864]{2,1,0:T(1,128)S(1)}, u32[]{:S(2)}, u32[]{:S(2)}) async-start(f32[8,1,36864]{2,1,0:T(1,128)} %reshape.61), calls=%async_computation.2 | async-start | bytes 2359296 | tf_op jit(solution)/shard_map/all_to_all | solution.py:49
  180.7 16.1 %all-to-all-done.2 = f32[8,1,36864]{2,1,0:T(1,128)S(1)} async-done(((f32[8,1,36864]{2,1,0:T(1,128)}), f32[8,1,36864]{2,1,0:T(1,128)S(1)}, u32[]{:S(2)}, u32[]{:S(2)}) %all-to-all-start.2) | async-done | bytes 1179680 | tf_op jit(solution)/shard_map/all_to_all | solution.py:49
  200.9 7.2 %reshape.62 = f32[768,16,24]{2,1,0:T(8,128)} reshape(f32[8,36864]{1,0:T(8,128)S(1)} %reduce.4) | data formatting | bytes 2359296
  208.0 5.8 %copy.31 = f32[16,24,8,96]{3,1,0,2:T(8,128)} copy(f32[16,24,8,96]{1,0,3,2:T(8,128)} %bitcast.89) | data formatting | bytes 2359296 | tf_op jit(solution)/shard_map/all_to_all | solution.py:49
  226.2 16.9 %all_to_all.122 = bf16[128,24,96]{2,1,0:T(8,128)(2,1)S(1)} all-to-all(bf16[128,24,96]{2,1,0:T(8,128)(2,1)S(1)} %copy.38), channel_id=1, replica_groups=mesh['band'=32,'hid'=8] {'hid'}, dimensions={0} | all-to-all | bytes 1179648 | tf_op jit(solution)/shard_map/all_to_all | solution.py:73
  245.6 16.0 %all_to_all.123 = bf16[128,24,96]{2,1,0:T(8,128)(2,1)S(1)} all-to-all(bf16[128,24,96]{2,1,0:T(8,128)(2,1)S(1)} %copy.33), channel_id=1, replica_groups=mesh['band'=32,'hid'=8] {'hid'}, dimensions={0} | all-to-all | bytes 1179648 | tf_op jit(solution)/shard_map/all_to_all | solution.py:72
  265.4 5.8 %reshape.63 = bf16[32,2,4608]{2,1,0:T(2,128)(2,1)S(1)} reshape(bf16[768,16,24]{2,1,0:T(8,128)(2,1)} %bitcast.92) | data formatting | bytes 1179648
  271.2 29.5 %all_to_all.124 = bf16[32,2,4608]{2,1,0:T(2,128)(2,1)S(1)} all-to-all(bf16[32,2,4608]{2,1,0:T(2,128)(2,1)S(1)} %reshape.63), channel_id=1, replica_groups=mesh['band'=32,'hid'=8] {'band'}, dimensions={0} | all-to-all | bytes 1179648 | tf_op jit(solution)/shard_map/all_to_all | solution.py:38
  300.6 5.7 %reshape.64 = bf16[768,16,24]{2,1,0:T(8,128)(2,1)} reshape(bf16[32,2,4608]{2,1,0:T(2,128)(2,1)S(1)} %all_to_all.124) | data formatting | bytes 1179648
  306.3 5.7 %copy.37 = bf16[16,32,24,24]{2,1,3,0:T(8,128)(2,1)} copy(bf16[16,32,24,24]{2,0,3,1:T(8,128)(2,1)} %bitcast.91) | data formatting | bytes 1179648 | tf_op jit(solution)/shard_map/all_to_all | solution.py:38
  312.0 5.3 %all_to_all.105 = bf16[16,768,24]{1,2,0:T(8,128)(2,1)S(1)} reshape(bf16[16,32,24,24]{2,1,3,0:T(8,128)(2,1)} %copy.37) | data formatting | bytes 1179648 | tf_op jit(solution)/shard_map/all_to_all | solution.py:38
  317.3 48.6 %all-gather.5.cloned.1.call-done = bf16[16,768,768]{2,1,0:T(8,128)(2,1)} async-done(((bf16[16,24,768]{2,1,0:T(8,128)(2,1)}), bf16[16,768,768]{2,1,0:T(8,128)(2,1)}) %all-gather.5.cloned.1.call-update) | async-done | bytes 18874384 | tf_op jit(solution)/shard_map/all_gather | solution.py:41
  365.9 7.7 %fusion.76 = f32[16,24,768]{2,1,0:T(8,128)S(1)} fusion(bf16[16,768,24]{1,2,0:T(8,128)(2,1)S(1)} %all_to_all.105, bf16[16,768,768]{2,1,0:T(8,128)(2,1)} %all-gather.5.cloned.1.call-done), kind=kOutput, calls=%fused_computation.97 | convolution fusion | flops 452984832 | bytes 20643840 | tf_op jit(solution)/shard_map/dot_general | solution.py:39
  378.6 7.4 %reshape.65 = f32[8,1,36864]{2,1,0:T(1,128)} reshape(f32[768,16,24]{2,1,0:T(8,128)} %bitcast.88) | data formatting | bytes 2359296
  386.0 7.0 %all-to-all-start.6 = ((f32[8,1,36864]{2,1,0:T(1,128)}), f32[8,1,36864]{2,1,0:T(1,128)S(1)}, u32[]{:S(2)}, u32[]{:S(2)}) async-start(f32[8,1,36864]{2,1,0:T(1,128)} %reshape.65), calls=%async_computation.6 | async-start | bytes 2359296 | tf_op jit(solution)/shard_map/all_to_all | solution.py:49
  395.5 16.1 %all-to-all-done.6 = f32[8,1,36864]{2,1,0:T(1,128)S(1)} async-done(((f32[8,1,36864]{2,1,0:T(1,128)}), f32[8,1,36864]{2,1,0:T(1,128)S(1)}, u32[]{:S(2)}, u32[]{:S(2)}) %all-to-all-start.6) | async-done | bytes 1179680 | tf_op jit(solution)/shard_map/all_to_all | solution.py:49
  415.1 7.2 %reshape.66 = f32[768,16,24]{2,1,0:T(8,128)} reshape(f32[8,36864]{1,0:T(8,128)S(1)} %reduce.5) | data formatting | bytes 2359296
  422.3 5.0 %copy.41 = f32[16,24,8,96]{3,1,0,2:T(8,128)S(1)} copy(f32[16,24,8,96]{1,0,3,2:T(8,128)} %bitcast.90) | data formatting | bytes 2359296 | tf_op jit(solution)/shard_map/all_to_all | solution.py:49
  (79 shorter events, 55.6 us)
Async XLA Ops:
  6.5 5.0 %copy-start = (f32[24,96,128]{2,1,0:T(8,128)S(1)}, f32[24,96,128]{2,1,0:T(8,128)}, u32[]{:S(2)}) copy-start(f32[24,96,128]{2,1,0:T(8,128)} %param.7) | copy-start | bytes 3538948
  6.5 143.6 %all-gather.3.cloned.1.call-start = ((), (), s32[]{:S(2)}) async-start(), calls=%async_computation.7 | async-start | bytes 19464192 | tf_op jit(solution)/shard_map/all_gather | solution.py:31
  9.7 2.7 copy-start.4
  12.3 4.0 copy-start.12
  12.3 4.0 copy-start.14
  16.4 0.8 copy-start.8
  171.4 6.9 %copy-start.13 = (f32[24,96]{1,0:T(8,128)S(1)}, f32[24,96]{1,0:T(8,128)}, u32[]{:S(2)}) copy-start(f32[24,96]{1,0:T(8,128)} %copy-done.12) | copy-start | bytes 27652
  171.4 6.9 %copy-start.15 = (f32[2,128,128]{2,1,0:T(8,128)S(1)}, f32[2,128,128]{2,1,0:T(8,128)}, u32[]{:S(2)}) copy-start(f32[2,128,128]{2,1,0:T(8,128)} %param.12) | copy-start | bytes 393220
  171.4 25.5 %all-to-all-start.2 = ((f32[8,1,36864]{2,1,0:T(1,128)}), f32[8,1,36864]{2,1,0:T(1,128)S(1)}, u32[]{:S(2)}, u32[]{:S(2)}) async-start(f32[8,1,36864]{2,1,0:T(1,128)} %reshape.61), calls=%async_computation.2 | async-start | bytes 2359296 | tf_op jit(solution)/shard_map/all_to_all | solution.py:49
  178.2 187.7 %all-gather.5.cloned.1.call-start = ((), (), s32[]{:S(2)}) async-start(), calls=%async_computation.8 | async-start | bytes 19464192 | tf_op jit(solution)/shard_map/all_gather | solution.py:41
  213.9 1.9 copy-start.1
  215.7 1.3 copy-start.3
  215.7 1.3 copy-start.6
  220.0 1.0 copy-start.5
  221.0 3.9 copy-start.10
  221.0 3.9 copy-start.9
  386.0 7.1 %copy-start.11 = (f32[24,96]{1,0:T(8,128)S(1)}, f32[24,96]{1,0:T(8,128)}, u32[]{:S(2)}) copy-start(f32[24,96]{1,0:T(8,128)} %copy-done.10) | copy-start | bytes 27652
  386.0 7.1 %copy-start.16 = (f32[2,128,128]{2,1,0:T(8,128)S(1)}, f32[2,128,128]{2,1,0:T(8,128)}, u32[]{:S(2)}) copy-start(f32[2,128,128]{2,1,0:T(8,128)} %param.12) | copy-start | bytes 393220
  386.0 25.7 %all-to-all-start.6 = ((f32[8,1,36864]{2,1,0:T(1,128)}), f32[8,1,36864]{2,1,0:T(1,128)S(1)}, u32[]{:S(2)}, u32[]{:S(2)}) async-start(f32[8,1,36864]{2,1,0:T(1,128)} %reshape.65), calls=%async_computation.6 | async-start | bytes 2359296 | tf_op jit(solution)/shard_map/all_to_all | solution.py:49
  427.6 1.3 copy-start.2
  427.6 1.3 copy-start.7
Sparse Core Ops, SparseCore 0:
  40.5 109.5 all-gather.2
  245.2 120.5 all-gather.4
where the time goes:
time: 446 us; the launch traced here: 440 us
  waiting for transfers between devices  173 us (39%)
  blocking collectives  99.2 us (22%)
  local copies, waits for them, and re-layouts  89 us (20%)
  matrix products  36.1 us (8%)
  other arithmetic  14.4 us (3%)
  starting transfers between devices  13.9 us (3%)
  between operations  13.9 us (3%)
    all_gather x1, waiting for transfers between devices, outgoing(): lax.all_gather(right, 'band', axis=1, tiled=True)  92.1 us
    all_gather x1, waiting for transfers between devices, incoming(): lax.all_gather(right, 'band', axis=1, tiled=True)  48.6 us
    unnamed x40, local copies, waits for them, and re-layouts  43 us
    all_to_all x2, blocking collectives, on_device(): lax.all_to_all(right, 'hid', split_axis=0, concat_axis=2, tiled=True)  37.7 us
    all_to_all x2, waiting for transfers between devices, finish(): lax.all_to_all(tri, 'hid', split_axis=2, concat_axis=0, tiled=True)  32.3 us
    all_to_all x2, blocking collectives, on_device(): lax.all_to_all(left, 'hid', split_axis=0, concat_axis=2, tiled=True)  32 us
    all_to_all x1, blocking collectives, incoming(): lax.all_to_all(left, 'band', split_axis=2, concat_axis=1, tiled=True)  29.5 us
    all_to_all x2, starting transfers between devices, finish(): lax.all_to_all(tri, 'hid', split_axis=2, concat_axis=0, tiled=True)  13.9 us
  transfers between devices with their start and end apart: 4, of which 4 were waited for; matrix products, arithmetic and copies ran while one was open for 6% of the time, Pallas kernels for 0%

commit v1 on v0

--- a/solution.py
+++ b/solution.py
@@ -5,6 +5,11 @@
 
 EPS = 1e-05
 HIGH = lax.Precision.HIGHEST
+
+
+def swapped_in(x, axis, d):
+    repeated = jnp.stack([x] * lax.axis_size(axis))
+    return jnp.concatenate(lax.all_to_all(repeated, axis, 0, 0), axis=d)
 
 
 def normalize(values):
@@ -38,7 +43,7 @@
     columns = lax.all_to_all(left, "band", split_axis=2, concat_axis=1, tiled=True)
     return lax.dot_general(
         columns,
-        lax.all_gather(right, "band", axis=1, tiled=True),
+        swapped_in(right, "band", 1),
         (((1,), (1,)), ((0,), (0,))),
         preferred_element_type=jnp.float32,
     )

time: 446 us -> 793 us (1.78)
  the two profiles are of different devices: /device:TPU:96 before, /device:TPU:1 now
where the time goes in v1:
time: 793 us; the launch traced here: 786 us
  waiting for transfers between devices  551 us (69%)
  local copies, waits for them, and re-layouts  107 us (13%)
  blocking collectives  34.7 us (4%)
  starting transfers between devices  33.4 us (4%)
  matrix products  30.9 us (4%)
  other arithmetic  14.3 us (2%)
  between operations  14 us (2%)
    all_to_all x1, waiting for transfers between devices, swapped_in(): return jnp.concatenate(lax.all_to_all(repeated, axis, 0, 0), axis=d)  394 us
    all_gather x1, waiting for transfers between devices, outgoing(): lax.all_gather(right, 'band', axis=1, tiled=True)  95.7 us
    unnamed x40, local copies, waits for them, and re-layouts  43.6 us
    all_to_all x2, waiting for transfers between devices, finish(): lax.all_to_all(tri, 'hid', split_axis=2, concat_axis=0, tiled=True)  30.4 us
    all_to_all x1, blocking collectives, on_device(): lax.all_to_all(right, 'hid', split_axis=0, concat_axis=2, tiled=True)  19.8 us
    all_to_all x1, waiting for transfers between devices, incoming(): lax.all_to_all(left, 'band', split_axis=2, concat_axis=1, tiled=True)  17 us
  transfers between devices with their start and end apart: 7, of which 7 were waited for; matrix products, arithmetic and copies ran while one was open for 4% of the time, Pallas kernels for 0%

profile of v1, /device:TPU:1, one launch (start us, length us, event | category | flops | bytes accessed | tf_op | source)
XLA Modules:
  0.0 785.5 jit_solution(8897681517351206196)
XLA Ops:
  17.6 19.8 %all_to_all.122 = bf16[128,24,96]{2,1,0:T(8,128)(2,1)S(1)} all-to-all(bf16[128,24,96]{2,1,0:T(8,128)(2,1)S(1)} %copy.27), channel_id=1, replica_groups=mesh['band'=32,'hid'=8] {'hid'}, dimensions={0} | all-to-all | bytes 1179648 | tf_op jit(solution)/shard_map/all_to_all | solution.py:78
  39.9 14.8 %all_to_all.123 = bf16[128,24,96]{2,1,0:T(8,128)(2,1)S(1)} all-to-all(bf16[128,24,96]{2,1,0:T(8,128)(2,1)S(1)} %copy.25), channel_id=1, replica_groups=mesh['band'=32,'hid'=8] {'hid'}, dimensions={0} | all-to-all | bytes 1179648 | tf_op jit(solution)/shard_map/all_to_all | solution.py:77
  55.9 95.7 %all-gather.2.cloned.1.call-done = bf16[16,768,768]{2,1,0:T(8,128)(2,1)} async-done(((bf16[16,24,768]{2,1,0:T(8,128)(2,1)}), bf16[16,768,768]{2,1,0:T(8,128)(2,1)}) %all-gather.2.cloned.1.call-update) | async-done | bytes 18874384 | tf_op jit(solution)/shard_map/all_gather | solution.py:36
  151.6 8.9 %fusion.75 = f32[16,24,768]{2,1,0:T(8,128)S(1)} fusion(bf16[16,24,768]{2,1,0:T(8,128)(2,1)S(1)} %all_to_all.91, bf16[16,768,768]{2,1,0:T(8,128)(2,1)} %all-gather.2.cloned.1.call-done), kind=kOutput, calls=%fused_computation.96 | convolution fusion | flops 452984832 | bytes 20643840 | tf_op jit(solution)/shard_map/dot_general | solution.py:34
  165.5 7.3 reshape.72
  172.8 6.2 all-to-all-start.2
  181.5 15.4 %all-to-all-done.2 = f32[8,1,36864]{2,1,0:T(1,128)S(1)} async-done(((f32[8,1,36864]{2,1,0:T(1,128)}), f32[8,1,36864]{2,1,0:T(1,128)S(1)}, u32[]{:S(2)}, u32[]{:S(2)}) %all-to-all-start.2) | async-done | bytes 1179680 | tf_op jit(solution)/shard_map/all_to_all | solution.py:54
  200.7 7.2 reshape.73
  207.9 6.0 copy.30
  232.0 11.4 %all-to-all-done.3 = bf16[128,24,96]{2,1,0:T(8,128)(2,1)S(1)} async-done(((bf16[128,24,96]{2,1,0:T(8,128)(2,1)}), bf16[128,24,96]{2,1,0:T(8,128)(2,1)S(1)}, u32[]{:S(2)}, u32[]{:S(2)}) %all-to-all-start.3) | async-done | bytes 589856 | tf_op jit(solution)/shard_map/all_to_all | solution.py:77
  251.1 6.4 reshape.74
  260.1 8.8 %all-to-all-start.4 = ((bf16[32,2,4608]{2,1,0:T(2,128)(2,1)}), bf16[32,2,4608]{2,1,0:T(2,128)(2,1)S(1)}, u32[]{:S(2)}, u32[]{:S(2)}) async-start(bf16[32,2,4608]{2,1,0:T(2,128)(2,1)} %reshape.74), calls=%async_computation.4 | async-start | bytes 1179648 | tf_op jit(solution)/shard_map/all_to_all | solution.py:43
  270.1 17.0 %all-to-all-done.4 = bf16[32,2,4608]{2,1,0:T(2,128)(2,1)S(1)} async-done(((bf16[32,2,4608]{2,1,0:T(2,128)(2,1)}), bf16[32,2,4608]{2,1,0:T(2,128)(2,1)S(1)}, u32[]{:S(2)}, u32[]{:S(2)}) %all-to-all-start.4) | async-done | bytes 589856 | tf_op jit(solution)/shard_map/all_to_all | solution.py:43
  287.0 6.9 stack.5
  293.9 6.3 all-to-all-start.6
  300.2 5.7 reshape.75
  305.9 5.6 copy.36
  311.5 5.3 all_to_all.106
  316.7 394.3 %all-to-all-done.6 = bf16[32,16,24,768]{3,2,1,0:T(8,128)(2,1)} async-done(((bf16[32,16,24,768]{3,2,1,0:T(8,128)(2,1)}), bf16[32,16,24,768]{3,2,1,0:T(8,128)(2,1)}, u32[]{:S(2)}, u32[]{:S(2)}) %all-to-all-start.6) | async-done | bytes 18874400 | tf_op jit(solution)/shard_map/all_to_all | solution.py:12
  711.0 9.5 %copy.39 = bf16[16,32,24,768]{3,2,1,0:T(8,128)(2,1)S(1)} copy(bf16[16,32,24,768]{3,2,0,1:T(8,128)(2,1)} %bitcast.27) | data formatting | bytes 37748736 | tf_op jit(solution)/shard_map/reshape | solution.py:12
  728.1 7.3 reshape.76
  742.6 15.0 %all-to-all-done.7 = f32[8,1,36864]{2,1,0:T(1,128)S(1)} async-done(((f32[8,1,36864]{2,1,0:T(1,128)}), f32[8,1,36864]{2,1,0:T(1,128)S(1)}, u32[]{:S(2)}, u32[]{:S(2)}) %all-to-all-start.7) | async-done | bytes 1179680 | tf_op jit(solution)/shard_map/all_to_all | solution.py:54
  761.0 7.2 reshape.77
  768.2 5.0 copy.41
  (83 shorter events, 78.6 us)
Async XLA Ops:
  6.5 5.0 copy-start
  6.5 145.0 %all-gather.2.cloned.1.call-start = ((), (), s32[]{:S(2)}) async-start(), calls=%async_computation.8 | async-start | bytes 19464192 | tf_op jit(solution)/shard_map/all_gather | solution.py:36
  9.7 2.7 copy-start.4
  12.3 4.0 copy-start.12
  12.3 4.0 copy-start.14
  16.4 0.8 copy-start.8
  172.8 6.2 copy-start.13
  172.8 6.2 copy-start.15
  172.8 24.1 %all-to-all-start.2 = ((f32[8,1,36864]{2,1,0:T(1,128)}), f32[8,1,36864]{2,1,0:T(1,128)S(1)}, u32[]{:S(2)}, u32[]{:S(2)}) async-start(f32[8,1,36864]{2,1,0:T(1,128)} %reshape.72), calls=%async_computation.2 | async-start | bytes 2359296 | tf_op jit(solution)/shard_map/all_to_all | solution.py:54
  214.0 1.9 copy-start.1
  215.8 1.3 copy-start.3
  215.8 1.3 copy-start.6
  220.1 1.0 copy-start.5
  221.1 3.9 copy-start.10
  221.1 3.9 copy-start.9
  227.1 16.3 %all-to-all-start.3 = ((bf16[128,24,96]{2,1,0:T(8,128)(2,1)}), bf16[128,24,96]{2,1,0:T(8,128)(2,1)S(1)}, u32[]{:S(2)}, u32[]{:S(2)}) async-start(bf16[128,24,96]{2,1,0:T(8,128)(2,1)} %copy.32), calls=%async_computation.3 | async-start | bytes 1572864 | tf_op jit(solution)/shard_map/all_to_all | solution.py:77
  243.4 16.7 %all-to-all-start.5 = ((bf16[128,24,96]{2,1,0:T(8,128)(2,1)}), bf16[128,24,96]{2,1,0:T(8,128)(2,1)S(1)}, u32[]{:S(2)}, u32[]{:S(2)}) async-start(bf16[128,24,96]{2,1,0:T(8,128)(2,1)} %copy.37), calls=%async_computation.5 | async-start | bytes 1572864 | tf_op jit(solution)/shard_map/all_to_all | solution.py:78
  260.1 27.0 %all-to-all-start.4 = ((bf16[32,2,4608]{2,1,0:T(2,128)(2,1)}), bf16[32,2,4608]{2,1,0:T(2,128)(2,1)S(1)}, u32[]{:S(2)}, u32[]{:S(2)}) async-start(bf16[32,2,4608]{2,1,0:T(2,128)(2,1)} %reshape.74), calls=%async_computation.4 | async-start | bytes 1179648 | tf_op jit(solution)/shard_map/all_to_all | solution.py:43
  293.9 417.1 %all-to-all-start.6 = ((bf16[32,16,24,768]{3,2,1,0:T(8,128)(2,1)}), bf16[32,16,24,768]{3,2,1,0:T(8,128)(2,1)}, u32[]{:S(2)}, u32[]{:S(2)}) async-start(bf16[32,16,24,768]{3,2,1,0:T(8,128)(2,1)} %stack.5), calls=%async_computation.6 | async-start | bytes 37748736 | tf_op jit(solution)/shard_map/all_to_all | solution.py:12
  735.5 4.6 copy-start.11
  735.5 4.7 copy-start.16
  735.5 22.2 %all-to-all-start.7 = ((f32[8,1,36864]{2,1,0:T(1,128)}), f32[8,1,36864]{2,1,0:T(1,128)S(1)}, u32[]{:S(2)}, u32[]{:S(2)}) async-start(f32[8,1,36864]{2,1,0:T(1,128)} %reshape.76), calls=%async_computation.7 | async-start | bytes 2359296 | tf_op jit(solution)/shard_map/all_to_all | solution.py:54
  773.5 1.3 copy-start.2
  773.5 1.3 copy-start.7
Sparse Core Ops, SparseCore 0:
  39.6 111.9 all-gather.1
